TPU v7x, 32 devices: a whole 2x2x4 slice. The times are simulated.
32 devices in a mesh: atoms: 4 (over y, x), energy: 8 (over z, core).
Axes of the slice: x: 2, y: 2, z: 4, core: 2. Of those that a mesh axis runs over, the one named last changes fastest.
Arguments:
- retarded_green_blocks: bfloat16 [4, 24, 2, 384, 384], P('atoms', 'energy'), may hold values from -0.21875 to 0.21875
- contact_lesser_sigma: bfloat16 [4, 24, 2, 384, 384], P('atoms', 'energy'), may hold values from -6 to 6
- energy_counts: int32 [8], replicated, may hold values from 1 to 3, 15 in all
- phonon_shift: int32 [64], replicated, may hold values from 1 to 7
- phonon_weight: float32 [4, 64], replicated, may hold values from 0.01 to 0.1
Outputs:
- scattered: bfloat16 [4, 24, 2, 384, 384], P('atoms', 'energy')
Inputs may be any that keep to these rules, and one draw needn't show every extreme that they name: energy_counts sums to 15; its largest entry is exactly 3.
All inputs are finite; a program needn't handle non-finite values.
Results may differ from a plain program's by a relative error of at most 0.007.
Values may be sent and summed in bfloat16 or wider, within the bound.
A program may use at most 64 MiB of HBM per device.

v0:
```python
import jax
import jax.numpy as jnp
from jax import lax
from jax.sharding import PartitionSpec as P


def extended(value, sides, width):
    for axis, dim in sides:
        size, length = (lax.axis_size(axis), value.shape[dim])
        up = [(i, (i + 1) % size) for i in range(size - 1)]
        down = [(j, i) for i, j in up]
        last = lax.slice_in_dim(value, length - width, length, axis=dim)
        leading = lax.slice_in_dim(value, 0, width, axis=dim)
        before = lax.ppermute(last, axis, up)
        after = lax.ppermute(leading, axis, down)
        value = jnp.concatenate([before, value, after], axis=dim)
    return value


def complex_product(left, right):
    prods = jnp.einsum("spik,sqkj->spqij", left, right, preferred_element_type=jnp.float32)
    return jnp.stack([prods[:, 0, 0] - prods[:, 1, 1], prods[:, 0, 1] + prods[:, 1, 0]], axis=1)


def product_adjoint(left, right):
    prods = jnp.einsum("spik,sqjk->spqij", left, right, preferred_element_type=jnp.float32)
    return jnp.stack([prods[:, 0, 0] + prods[:, 1, 1], prods[:, 1, 0] - prods[:, 0, 1]], axis=1)


def kernels(energy_counts, phonon_shift, phonon_weight, groups, per_group):
    total_slots = groups * per_group
    starts = jnp.cumsum(energy_counts) - energy_counts
    start_slot = jnp.broadcast_to(starts[:, None], (groups, per_group)).reshape(total_slots)
    slot_tally = jnp.broadcast_to(energy_counts[:, None], (groups, per_group)).reshape(total_slots)
    within = jnp.arange(total_slots, dtype=jnp.int32) % per_group
    energy_index = start_slot + within
    live = (within < slot_tally).astype(jnp.float32)
    spacing = energy_index[None, :] - energy_index[:, None]
    upward = (spacing[:, :, None] == phonon_shift[None, None, :]).astype(jnp.float32)
    downward = (spacing[:, :, None] == -phonon_shift[None, None, :]).astype(jnp.float32)
    mask = live[:, None] * live[None, :]
    own_kernel = jnp.sum(upward * phonon_weight[0] + downward * phonon_weight[1], axis=-1) * mask
    side_kernel = jnp.sum(upward * phonon_weight[2] + downward * phonon_weight[3], axis=-1) * mask
    return (own_kernel.astype(jnp.bfloat16), side_kernel.astype(jnp.bfloat16))


def on_device(
    retarded_green_blocks, contact_lesser_sigma, energy_counts, phonon_shift, phonon_weight
):
    groups = lax.axis_size("energy")
    per_group = retarded_green_blocks.shape[1]
    retarded = retarded_green_blocks[0]
    mixed = complex_product(retarded, contact_lesser_sigma[0]).astype(jnp.bfloat16)
    lesser = product_adjoint(mixed, retarded).astype(jnp.bfloat16)[None]
    own_kernel, side_kernel = kernels(energy_counts, phonon_shift, phonon_weight, groups, per_group)
    moved = lax.all_to_all(lesser, "energy", split_axis=3, concat_axis=1, tiled=True)
    regrouped = extended(moved, (("atoms", 0),), 1)
    slot_count = regrouped.shape[1]
    columns = regrouped.shape[2] * regrouped.shape[3] * regrouped.shape[4]
    flat = regrouped.reshape(3, slot_count, columns)
    sigma = jnp.dot(own_kernel, flat[1], preferred_element_type=jnp.float32)
    sigma = sigma + jnp.dot(side_kernel, flat[0], preferred_element_type=jnp.float32)
    sigma = sigma + jnp.dot(side_kernel, flat[2], preferred_element_type=jnp.float32)
    sigma = sigma.astype(jnp.bfloat16).reshape((1,) + regrouped.shape[1:])
    returned = lax.all_to_all(sigma, "energy", split_axis=1, concat_axis=3, tiled=True)
    result = complex_product(retarded, returned[0]).astype(jnp.bfloat16)
    return result[None]


def solution(mesh):
    in_specs = (
        P("atoms", "energy", None, None, None),
        P("atoms", "energy", None, None, None),
        P(),
        P(),
        P(),
    )
    out_specs = P("atoms", "energy", None, None, None)
    return jax.shard_map(
        on_device, mesh=mesh, in_specs=in_specs, out_specs=out_specs, check_vma=False
    )
```

profile of v0, /device:TPU:0, one launch (start us, length us, event | category | flops | bytes accessed | tf_op | source)
XLA Modules:
  0.0 195.5 jit_solution(2721880612030138604)
XLA Ops:
  0.0 1.5 copy-done
  1.5 3.6 %convolution_bitcast_fusion.2 = f32[3,2,2,384,384]{3,4,1,2,0:T(8,128)S(1)} fusion(bf16[1,3,2,384,384]{4,3,2,1,0:T(8,128)(2,1)} %param.6, bf16[1,3,2,384,384]{4,3,2,1,0:T(8,128)(2,1)S(1)} %copy-done), kind=kOutput, calls=%fused_computation.5 | convolution fusion | flops 1358954496 | bytes 10616832 | tf_op jit(solution)/shard_map/spik,sqkj->spqij/dot_general | solution.py:21
  5.5 2.2 %convolution_bitcast_fusion.1 = f32[3,2,2,384,384]{4,3,2,1,0:T(8,128)S(1)} fusion(bf16[1,3,2,384,384]{4,3,2,1,0:T(8,128)(2,1)S(1)} %copy-done, bf16[3,1,384,384]{2,3,0,1:T(8,128)(2,1)S(1)} %fusion.16, bf16[3,1,384,384]{2,3,0,1:T(8,128)(2,1)S(1)} %fusion.15), kind=kOutput, calls=%fused_computation.4 | convolution fusion | flops 1359839232 | bytes 10616832 | tf_op jit(solution)/shard_map/spik,sqjk->spqij/dot_general | solution.py:26
  8.3 1.8 copy.90
  10.1 48.2 %all_to_all.33 = bf16[1,3,2,384,384]{4,2,1,0,3:T(2,128)(2,1)S(1)} all-to-all(bf16[1,3,2,384,384]{4,2,1,0,3:T(2,128)(2,1)S(1)} %copy.90), channel_id=1, replica_groups=mesh['atoms'=4,'energy'=8] {'energy'}, dimensions={3} | all-to-all | bytes 3538944 | tf_op jit(solution)/shard_map/all_to_all | solution.py:56
  58.8 4.6 %collective-permute-start = (bf16[1,24,2,48,384]{4,3,2,1,0:T(8,128)(2,1)S(1)}, bf16[1,24,2,48,384]{4,3,2,1,0:T(8,128)(2,1)}, u32[]{:S(2)}, u32[]{:S(2)}) collective-permute-start(bf16[1,24,2,48,384]{4,3,2,1,0:T(8,128)(2,1)S(1)} %bitcast.119), channel_id=1, source_target_pairs={{0,8},{8,16},{16,24},{1,9},{9,17},{17,25},{2,10},{10,18},{18,26},{... | collective-permute-start | bytes 5308424 | tf_op jit(solution)/shard_map/ppermute | solution.py:14
  63.4 0.5 neg.4
  64.2 0.6 reshape.326
  64.8 0.7 reshape.327
  65.5 1.3 collective-permute-start.1
  66.8 0.6 fusion.31
  67.5 1.6 fusion.24
  69.1 0.7 compare_convert_fusion
  69.8 2.2 %squeeze.14 = bf16[24,36864]{1,0:T(8,128)(2,1)} reshape(bf16[1,8,3,2,48,384]{5,4,3,2,1,0:T(8,128)(2,1)S(1)} %copy.92) | data formatting | bytes 3538944 | tf_op jit(solution)/shard_map/squeeze | solution.py:61
  72.0 4.0 %fusion.27 = f32[24,36864]{1,0:T(8,128)} fusion(bf16[24,36864]{1,0:T(8,128)(2,1)} %squeeze.14, f32[24,24]{1,0:T(8,128)} %get-tuple-element.6, f32[24]{0:T(128)S(1)} %compare_convert_fusion), kind=kOutput, calls=%fused_computation.50 | convolution fusion | flops 42469056 | bytes 5310816 | tf_op jit(solution)/shard_map/dot_general | solution.py:61
  76.0 23.7 %collective-permute-done = bf16[1,24,2,48,384]{4,3,2,1,0:T(8,128)(2,1)} collective-permute-done((bf16[1,24,2,48,384]{4,3,2,1,0:T(8,128)(2,1)S(1)}, bf16[1,24,2,48,384]{4,3,2,1,0:T(8,128)(2,1)}, u32[]{:S(2)}, u32[]{:S(2)}) %collective-permute-start) | collective-permute-done | bytes 1769504 | tf_op jit(solution)/shard_map/ppermute | solution.py:14
  99.7 3.9 %squeeze.15 = bf16[24,36864]{1,0:T(8,128)(2,1)} reshape(bf16[1,24,2,48,384]{4,3,2,1,0:T(8,128)(2,1)} %collective-permute-done) | data formatting | bytes 3538944 | tf_op jit(solution)/shard_map/squeeze | solution.py:62
  103.7 5.0 %convolution_add_fusion.1 = f32[24,36864]{1,0:T(8,128)} fusion(f32[24,36864]{1,0:T(8,128)} %fusion.27, bf16[24,36864]{1,0:T(8,128)(2,1)} %squeeze.15, f32[24,24]{1,0:T(8,128)S(1)} %get-tuple-element.5, f32[24]{0:T(128)S(1)} %compare_convert_fusion), kind=kOutput, calls=%fused_computation.1 | convolution fusion | flops 43353792 | bytes 8849760 | tf_op jit(solution)/shard_map/dot_general | solution.py:62
  108.7 31.0 %collective-permute-done.1 = bf16[1,24,2,48,384]{4,3,2,1,0:T(8,128)(2,1)} collective-permute-done((bf16[1,24,2,48,384]{4,3,2,1,0:T(8,128)(2,1)S(1)}, bf16[1,24,2,48,384]{4,3,2,1,0:T(8,128)(2,1)}, u32[]{:S(2)}, u32[]{:S(2)}) %collective-permute-start.1) | collective-permute-done | bytes 1769504 | tf_op jit(solution)/shard_map/ppermute | solution.py:15
  139.7 2.7 %squeeze.16 = bf16[24,36864]{1,0:T(8,128)(2,1)S(1)} reshape(bf16[1,24,2,48,384]{4,3,2,1,0:T(8,128)(2,1)} %collective-permute-done.1) | data formatting | bytes 3538944 | tf_op jit(solution)/shard_map/squeeze | solution.py:63
  142.4 2.7 %fusion = bf16[24,36864]{1,0:T(8,128)(2,1)S(1)} fusion(f32[24,36864]{1,0:T(8,128)} %convolution_add_fusion.1, bf16[24,36864]{1,0:T(8,128)(2,1)S(1)} %squeeze.16, f32[24,24]{1,0:T(8,128)S(1)} %get-tuple-element.5, f32[24]{0:T(128)S(1)} %compare_convert_fusion), kind=kOutput, calls=%fused_computation.2 | convolution fusion | flops 44238528 | bytes 7080288 | tf_op jit(solution)/shard_map/dot_general | solution.py:63
  145.3 44.9 %all_to_all.34 = bf16[1,24,2,48,384]{4,3,2,0,1:T(8,128)(2,1)S(1)} all-to-all(bf16[1,24,2,48,384]{4,3,2,0,1:T(8,128)(2,1)S(1)} %bitcast.122), channel_id=1, replica_groups=mesh['atoms'=4,'energy'=8] {'energy'}, dimensions={1} | all-to-all | bytes 3538944 | tf_op jit(solution)/shard_map/all_to_all | solution.py:65
  190.4 2.2 %convolution_bitcast_fusion = f32[3,2,2,384,384]{3,4,1,2,0:T(8,128)S(1)} fusion(bf16[3,2,384,384,1]{3,2,4,1,0:T(8,128)(2,1)S(1)} %bitcast.125, bf16[1,3,2,384,384]{4,3,2,1,0:T(8,128)(2,1)S(1)} %copy-done), kind=kOutput, calls=%fused_computation.3 | convolution fusion | flops 1358954496 | bytes 10616832 | tf_op jit(solution)/shard_map/spik,sqkj->spqij/dot_general | solution.py:21
  193.2 2.3 %copy.99 = bf16[1,3,2,384,384]{4,3,2,1,0:T(8,128)(2,1)} copy(bf16[1,3,2,384,384]{3,4,1,2,0:T(8,128)(2,1)S(1)} %pad_maximum_fusion.1) | data formatting | bytes 3538944 | tf_op jit(solution)/shard_map/stack | solution.py:22
  (25 shorter events, 2.8 us)
Async XLA Ops:
  0.0 1.5 copy-start
  58.5 4.9 %copy-start.2 = (s32[64]{0:T(128)S(1)}, s32[64]{0:T(128)}, u32[]{:S(2)}) copy-start(s32[64]{0:T(128)} %param.8) | copy-start | bytes 772
  58.6 5.4 %copy-start.3 = (s32[8]{0:T(128)S(1)}, s32[8]{0:T(128)}, u32[]{:S(2)}) copy-start(s32[8]{0:T(128)} %param.7) | copy-start | bytes 100
  58.6 8.8 %copy-start.1 = (f32[4,64]{1,0:T(4,128)S(1)}, f32[4,64]{1,0:T(4,128)}, u32[]{:S(2)}) copy-start(f32[4,64]{1,0:T(4,128)} %param.9) | copy-start | bytes 3076
  58.8 41.0 %collective-permute-start = (bf16[1,24,2,48,384]{4,3,2,1,0:T(8,128)(2,1)S(1)}, bf16[1,24,2,48,384]{4,3,2,1,0:T(8,128)(2,1)}, u32[]{:S(2)}, u32[]{:S(2)}) collective-permute-start(bf16[1,24,2,48,384]{4,3,2,1,0:T(8,128)(2,1)S(1)} %bitcast.119), channel_id=1, source_target_pairs={{0,8},{8,16},{16,24},{1,9},{9,17},{17,25},{2,10},{10,18},{18,26},{... | collective-permute-start | bytes 5308424 | tf_op jit(solution)/shard_map/ppermute | solution.py:14
  65.5 74.2 %collective-permute-start.1 = (bf16[1,24,2,48,384]{4,3,2,1,0:T(8,128)(2,1)S(1)}, bf16[1,24,2,48,384]{4,3,2,1,0:T(8,128)(2,1)}, u32[]{:S(2)}, u32[]{:S(2)}) collective-permute-start(bf16[1,24,2,48,384]{4,3,2,1,0:T(8,128)(2,1)S(1)} %bitcast.120), channel_id=1, source_target_pairs={{8,0},{16,8},{24,16},{9,1},{17,9},{25,17},{10,2},{18,10},{26,18},{... | collective-permute-start | bytes 5308424 | tf_op jit(solution)/shard_map/ppermute | solution.py:15
where the time goes:
time: 196 us; the launch traced here: 195 us
  blocking collectives  93 us (47%)
  waiting for transfers between devices  54.8 us (28%)
  matrix products  19.8 us (10%)
  local copies, waits for them, and re-layouts  16.6 us (8%)
  starting transfers between devices  5.92 us (3%)
  other arithmetic  5.25 us (3%)
    all_to_all x1, blocking collectives, on_device(): lax.all_to_all(lesser, 'energy', split_axis=3, concat_axis=1, tiled=True)  48.2 us
    all_to_all x1, blocking collectives, on_device(): lax.all_to_all(sigma, 'energy', split_axis=1, concat_axis=3, tiled=True)  44.9 us
    ppermute x1, waiting for transfers between devices, extended(): after = lax.ppermute(leading, axis, down)  31 us
    ppermute x1, waiting for transfers between devices, extended(): before = lax.ppermute(last, axis, up)  23.7 us
    dot_general x2, matrix products, complex_product(): jnp.einsum('spik,sqkj->spqij', left, right, preferred_element_type=jnp.fl...  5.83 us
    dot_general x1, matrix products, on_device(): jnp.dot(side_kernel, flat[0], preferred_element_type=jnp.float32)  5.02 us
    ppermute x1, starting transfers between devices, extended(): before = lax.ppermute(last, axis, up)  4.64 us
    dot_general x1, matrix products, on_device(): sigma = jnp.dot(own_kernel, flat[1], preferred_element_type=jnp.float32)  4.04 us
  transfers between devices with their start and end apart: 2, of which 2 were waited for; matrix products, arithmetic and copies ran while one was open for 10% of the time, Pallas kernels for 0%

commit v1 on v0

--- a/solution.py
+++ b/solution.py
@@ -62,7 +62,15 @@
     sigma = sigma + jnp.dot(side_kernel, flat[0], preferred_element_type=jnp.float32)
     sigma = sigma + jnp.dot(side_kernel, flat[2], preferred_element_type=jnp.float32)
     sigma = sigma.astype(jnp.bfloat16).reshape((1,) + regrouped.shape[1:])
-    returned = lax.all_to_all(sigma, "energy", split_axis=1, concat_axis=3, tiled=True)
+    ways, here = (lax.axis_size("energy"), lax.axis_index("energy"))
+    width_2 = sigma.shape[1] // ways
+    turned = jnp.roll(sigma, -here * width_2, axis=1)
+    got = [lax.slice_in_dim(turned, 0, width_2, axis=1)]
+    for far in range(1, ways):
+        sent = lax.slice_in_dim(turned, far * width_2, (far + 1) * width_2, axis=1)
+        got.append(lax.ppermute(sent, "energy", [(d, (d + far) % ways) for d in range(ways)]))
+    line = jnp.concatenate(got[::-1], axis=3)
+    returned = jnp.roll(line, (here + 1) * got[0].shape[3], axis=3)
     result = complex_product(retarded, returned[0]).astype(jnp.bfloat16)
     return result[None]
 

time: 196 us -> 194 us (0.990)
  blocking collectives: 93 us -> 48.2 us
  waiting for transfers between devices: 54.8 us -> 85.8 us
  local copies, waits for them, and re-layouts: 16.6 us -> 21.9 us
  starting transfers between devices: 5.92 us -> 11.2 us
    all_to_all x1 -> x0, blocking collectives: 44.9 us -> none  [on_device(): lax.all_to_all(sigma, 'energy', split_axis=1, concat_axis=3, tiled=True)]
    ppermute x0 -> x7, waiting for transfers between devices: none -> 31.2 us  [on_device(): lax.ppermute(sent, 'energy', [(d, (d + far) % ways) for d in range(ways)])]
    ppermute x0 -> x7, starting transfers between devices: none -> 5.15 us  [on_device(): lax.ppermute(sent, 'energy', [(d, (d + far) % ways) for d in range(ways)])]
    unnamed x9 -> x24, local copies, waits for them, and re-layouts: 1.74 us -> 6.03 us
  transfers between devices with their start and end apart: 2 -> 9, of which waited for: 2 -> 6; matrix products, arithmetic and copies ran while one was open for 10% -> 12% of each run, Pallas kernels for 0% -> 0%
where the time goes in v1:
time: 194 us; the launch traced here: 193 us
  waiting for transfers between devices  85.8 us (44%)
  blocking collectives  48.2 us (25%)
  local copies, waits for them, and re-layouts  21.9 us (11%)
  matrix products  19.8 us (10%)
  starting transfers between devices  11.2 us (6%)
  other arithmetic  5.99 us (3%)
    all_to_all x1, blocking collectives, on_device(): lax.all_to_all(lesser, 'energy', split_axis=3, concat_axis=1, tiled=True)  48.2 us
    ppermute x7, waiting for transfers between devices, on_device(): lax.ppermute(sent, 'energy', [(d, (d + far) % ways) for d in range(ways)])  31.2 us
    ppermute x1, waiting for transfers between devices, extended(): after = lax.ppermute(leading, axis, down)  31 us
    ppermute x1, waiting for transfers between devices, extended(): before = lax.ppermute(last, axis, up)  23.6 us
    unnamed x24, local copies, waits for them, and re-layouts  6.03 us
    dot_general x2, matrix products, complex_product(): jnp.einsum('spik,sqkj->spqij', left, right, preferred_element_type=jnp.fl...  5.85 us
    ppermute x7, starting transfers between devices, on_device(): lax.ppermute(sent, 'energy', [(d, (d + far) % ways) for d in range(ways)])  5.15 us
    dot_general x1, matrix products, on_device(): jnp.dot(side_kernel, flat[0], preferred_element_type=jnp.float32)  5.02 us
  transfers between devices with their start and end apart: 9, of which 6 were waited for; matrix products, arithmetic and copies ran while one was open for 12% of the time, Pallas kernels for 0%

profile of v1, /device:TPU:0, one launch (start us, length us, event | category | flops | bytes accessed | tf_op | source)
XLA Modules:
  0.0 193.2 jit_solution(10999405325502706671)
XLA Ops:
  0.0 1.5 copy-done
  1.5 3.6 %convolution_bitcast_fusion.2 = f32[3,2,2,384,384]{3,4,1,2,0:T(8,128)S(1)} fusion(bf16[1,3,2,384,384]{4,3,2,1,0:T(8,128)(2,1)} %param.6, bf16[1,3,2,384,384]{4,3,2,1,0:T(8,128)(2,1)S(1)} %copy-done), kind=kOutput, calls=%fused_computation.7 | convolution fusion | flops 1358954496 | bytes 10616832 | tf_op jit(solution)/shard_map/spik,sqkj->spqij/dot_general | solution.py:21
  5.5 2.2 %convolution_bitcast_fusion.1 = f32[3,2,2,384,384]{4,3,2,1,0:T(8,128)S(1)} fusion(bf16[1,3,2,384,384]{4,3,2,1,0:T(8,128)(2,1)S(1)} %copy-done, bf16[3,1,384,384]{2,3,0,1:T(8,128)(2,1)S(1)} %fusion.19, bf16[3,1,384,384]{2,3,0,1:T(8,128)(2,1)S(1)} %fusion.18), kind=kOutput, calls=%fused_computation.6 | convolution fusion | flops 1359839232 | bytes 10616832 | tf_op jit(solution)/shard_map/spik,sqjk->spqij/dot_general | solution.py:26
  8.3 1.8 copy.72
  10.1 48.2 %all_to_all.18 = bf16[1,3,2,384,384]{4,2,1,0,3:T(2,128)(2,1)S(1)} all-to-all(bf16[1,3,2,384,384]{4,2,1,0,3:T(2,128)(2,1)S(1)} %copy.72), channel_id=1, replica_groups=mesh['atoms'=4,'energy'=8] {'energy'}, dimensions={3} | all-to-all | bytes 3538944 | tf_op jit(solution)/shard_map/all_to_all | solution.py:56
  58.8 4.6 %collective-permute-start = (bf16[1,24,2,48,384]{4,3,2,1,0:T(8,128)(2,1)S(1)}, bf16[1,24,2,48,384]{4,3,2,1,0:T(8,128)(2,1)}, u32[]{:S(2)}, u32[]{:S(2)}) collective-permute-start(bf16[1,24,2,48,384]{4,3,2,1,0:T(8,128)(2,1)S(1)} %bitcast.115), channel_id=1, source_target_pairs={{0,8},{8,16},{16,24},{1,9},{9,17},{17,25},{2,10},{10,18},{18,26},{... | collective-permute-start | bytes 5308424 | tf_op jit(solution)/shard_map/ppermute | solution.py:14
  65.5 1.5 collective-permute-start.1
  67.7 1.6 fusion.27
  69.9 2.2 %squeeze.14 = bf16[24,36864]{1,0:T(8,128)(2,1)} reshape(bf16[1,8,3,2,48,384]{5,4,3,2,1,0:T(8,128)(2,1)S(1)} %copy.74) | data formatting | bytes 3538944 | tf_op jit(solution)/shard_map/squeeze | solution.py:61
  72.1 4.0 %fusion.30 = f32[24,36864]{1,0:T(8,128)} fusion(bf16[24,36864]{1,0:T(8,128)(2,1)} %squeeze.14, f32[24,24]{1,0:T(8,128)} %get-tuple-element.6, f32[24]{0:T(128)S(1)} %compare_convert_fusion), kind=kOutput, calls=%fused_computation.71 | convolution fusion | flops 42469056 | bytes 5310816 | tf_op jit(solution)/shard_map/dot_general | solution.py:61
  76.1 23.6 %collective-permute-done = bf16[1,24,2,48,384]{4,3,2,1,0:T(8,128)(2,1)} collective-permute-done((bf16[1,24,2,48,384]{4,3,2,1,0:T(8,128)(2,1)S(1)}, bf16[1,24,2,48,384]{4,3,2,1,0:T(8,128)(2,1)}, u32[]{:S(2)}, u32[]{:S(2)}) %collective-permute-start) | collective-permute-done | bytes 1769504 | tf_op jit(solution)/shard_map/ppermute | solution.py:14
  99.7 3.9 %squeeze.15 = bf16[24,36864]{1,0:T(8,128)(2,1)} reshape(bf16[1,24,2,48,384]{4,3,2,1,0:T(8,128)(2,1)} %collective-permute-done) | data formatting | bytes 3538944 | tf_op jit(solution)/shard_map/squeeze | solution.py:62
  103.7 5.0 %convolution_add_fusion.1 = f32[24,36864]{1,0:T(8,128)} fusion(f32[24,36864]{1,0:T(8,128)} %fusion.30, bf16[24,36864]{1,0:T(8,128)(2,1)} %squeeze.15, f32[24,24]{1,0:T(8,128)S(1)} %get-tuple-element.5, f32[24]{0:T(128)S(1)} %compare_convert_fusion), kind=kOutput, calls=%fused_computation.1 | convolution fusion | flops 43353792 | bytes 8849760 | tf_op jit(solution)/shard_map/dot_general | solution.py:62
  108.7 31.0 %collective-permute-done.1 = bf16[1,24,2,48,384]{4,3,2,1,0:T(8,128)(2,1)} collective-permute-done((bf16[1,24,2,48,384]{4,3,2,1,0:T(8,128)(2,1)S(1)}, bf16[1,24,2,48,384]{4,3,2,1,0:T(8,128)(2,1)}, u32[]{:S(2)}, u32[]{:S(2)}) %collective-permute-start.1) | collective-permute-done | bytes 1769504 | tf_op jit(solution)/shard_map/ppermute | solution.py:15
  139.7 2.7 %squeeze.16 = bf16[24,36864]{1,0:T(8,128)(2,1)S(1)} reshape(bf16[1,24,2,48,384]{4,3,2,1,0:T(8,128)(2,1)} %collective-permute-done.1) | data formatting | bytes 3538944 | tf_op jit(solution)/shard_map/squeeze | solution.py:63
  142.4 2.7 %fusion = bf16[24,36864]{1,0:T(8,128)(2,1)S(1)} fusion(f32[24,36864]{1,0:T(8,128)} %convolution_add_fusion.1, bf16[24,36864]{1,0:T(8,128)(2,1)S(1)} %squeeze.16, f32[24,24]{1,0:T(8,128)S(1)} %get-tuple-element.5, f32[24]{0:T(128)S(1)} %compare_convert_fusion), kind=kOutput, calls=%fused_computation.2 | convolution fusion | flops 44238528 | bytes 7080288 | tf_op jit(solution)/shard_map/dot_general | solution.py:63
  147.9 1.2 collective-permute-start.3
  149.9 3.4 %collective-permute-done.2 = bf16[1,3,2,48,384]{4,3,2,1,0:T(8,128)(2,1)} collective-permute-done((bf16[1,3,2,48,384]{4,3,2,1,0:T(8,128)(2,1)}, bf16[1,3,2,48,384]{4,3,2,1,0:T(8,128)(2,1)}, u32[]{:S(2)}, u32[]{:S(2)}) %collective-permute-start.2) | collective-permute-done | bytes 221216 | tf_op jit(solution)/shard_map/ppermute | solution.py:71
  153.3 2.5 %collective-permute-start.4 = (bf16[1,3,2,48,384]{4,3,2,1,0:T(8,128)(2,1)}, bf16[1,3,2,48,384]{4,3,2,1,0:T(8,128)(2,1)S(1)}, u32[]{:S(2)}, u32[]{:S(2)}) collective-permute-start(bf16[1,3,2,48,384]{4,3,2,1,0:T(8,128)(2,1)} %get-tuple-element.11), channel_id=1, source_target_pairs={{0,5},{1,6},{2,7},{3,0},{4,1},{5,2},{6,3},{7,4},{8,13},{9,14},{10,... | collective-permute-start | bytes 663560 | tf_op jit(solution)/shard_map/ppermute | solution.py:71
  156.8 11.3 %collective-permute-done.3 = bf16[1,3,2,48,384]{4,3,2,1,0:T(8,128)(2,1)} collective-permute-done((bf16[1,3,2,48,384]{4,3,2,1,0:T(8,128)(2,1)}, bf16[1,3,2,48,384]{4,3,2,1,0:T(8,128)(2,1)}, u32[]{:S(2)}, u32[]{:S(2)}) %collective-permute-start.3) | collective-permute-done | bytes 221216 | tf_op jit(solution)/shard_map/ppermute | solution.py:71
  169.1 3.2 %collective-permute-done.4 = bf16[1,3,2,48,384]{4,3,2,1,0:T(8,128)(2,1)S(1)} collective-permute-done((bf16[1,3,2,48,384]{4,3,2,1,0:T(8,128)(2,1)}, bf16[1,3,2,48,384]{4,3,2,1,0:T(8,128)(2,1)S(1)}, u32[]{:S(2)}, u32[]{:S(2)}) %collective-permute-start.4) | collective-permute-done | bytes 221216 | tf_op jit(solution)/shard_map/ppermute | solution.py:71
  172.4 13.2 %collective-permute-done.5 = bf16[1,3,2,48,384]{4,3,2,1,0:T(8,128)(2,1)S(1)} collective-permute-done((bf16[1,3,2,48,384]{4,3,2,1,0:T(8,128)(2,1)}, bf16[1,3,2,48,384]{4,3,2,1,0:T(8,128)(2,1)S(1)}, u32[]{:S(2)}, u32[]{:S(2)}) %collective-permute-start.5) | collective-permute-done | bytes 221216 | tf_op jit(solution)/shard_map/ppermute | solution.py:71
  188.1 2.2 %convolution_bitcast_fusion = f32[3,2,2,384,384]{3,4,1,2,0:T(8,128)S(1)} fusion(bf16[1,3,2,384,384]{4,3,2,1,0:T(8,128)(2,1)S(1)} %copy-done, bf16[1,3,2,768,384]{4,3,2,1,0:T(8,128)(2,1)S(1)} %slice_dynamic-update-slice_fusion.1, s32[]{:T(128)S(6)} %select_n.49), kind=kOutput, calls=%fused_computation.5 | convolution fusion | flops 1358954496 | bytes 10616836 | tf_op jit(solution)/shard_map/spik,sqkj->spqij/dot_general | solution.py:21
  190.9 2.3 %copy.79 = bf16[1,3,2,384,384]{4,3,2,1,0:T(8,128)(2,1)} copy(bf16[1,3,2,384,384]{3,4,1,2,0:T(8,128)(2,1)S(1)} %pad_maximum_fusion.1) | data formatting | bytes 3538944 | tf_op jit(solution)/shard_map/stack | solution.py:22
  (55 shorter events, 13.4 us)
Async XLA Ops:
  0.0 1.5 copy-start
  58.5 4.8 %copy-start.3 = (s32[8]{0:T(128)S(1)}, s32[8]{0:T(128)}, u32[]{:S(2)}) copy-start(s32[8]{0:T(128)} %param.7) | copy-start | bytes 100
  58.6 5.0 %copy-start.2 = (s32[64]{0:T(128)S(1)}, s32[64]{0:T(128)}, u32[]{:S(2)}) copy-start(s32[64]{0:T(128)} %param.8) | copy-start | bytes 772
  58.6 9.1 %copy-start.1 = (f32[4,64]{1,0:T(4,128)S(1)}, f32[4,64]{1,0:T(4,128)}, u32[]{:S(2)}) copy-start(f32[4,64]{1,0:T(4,128)} %param.9) | copy-start | bytes 3076
  58.8 41.0 %collective-permute-start = (bf16[1,24,2,48,384]{4,3,2,1,0:T(8,128)(2,1)S(1)}, bf16[1,24,2,48,384]{4,3,2,1,0:T(8,128)(2,1)}, u32[]{:S(2)}, u32[]{:S(2)}) collective-permute-start(bf16[1,24,2,48,384]{4,3,2,1,0:T(8,128)(2,1)S(1)} %bitcast.115), channel_id=1, source_target_pairs={{0,8},{8,16},{16,24},{1,9},{9,17},{17,25},{2,10},{10,18},{18,26},{... | collective-permute-start | bytes 5308424 | tf_op jit(solution)/shard_map/ppermute | solution.py:14
  65.5 74.2 %collective-permute-start.1 = (bf16[1,24,2,48,384]{4,3,2,1,0:T(8,128)(2,1)S(1)}, bf16[1,24,2,48,384]{4,3,2,1,0:T(8,128)(2,1)}, u32[]{:S(2)}, u32[]{:S(2)}) collective-permute-start(bf16[1,24,2,48,384]{4,3,2,1,0:T(8,128)(2,1)S(1)} %bitcast.116), channel_id=1, source_target_pairs={{8,0},{16,8},{24,16},{9,1},{17,9},{25,17},{10,2},{18,10},{26,18},{... | collective-permute-start | bytes 5308424 | tf_op jit(solution)/shard_map/ppermute | solution.py:15
  147.3 6.1 %collective-permute-start.2 = (bf16[1,3,2,48,384]{4,3,2,1,0:T(8,128)(2,1)}, bf16[1,3,2,48,384]{4,3,2,1,0:T(8,128)(2,1)}, u32[]{:S(2)}, u32[]{:S(2)}) collective-permute-start(bf16[1,3,2,48,384]{4,3,2,1,0:T(8,128)(2,1)} %get-tuple-element.13), channel_id=1, source_target_pairs={{0,7},{1,0},{2,1},{3,2},{4,3},{5,4},{6,5},{7,6},{8,15},{9,8},{10,9... | collective-permute-start | bytes 663560 | tf_op jit(solution)/shard_map/ppermute | solution.py:71
  147.9 20.3 %collective-permute-start.3 = (bf16[1,3,2,48,384]{4,3,2,1,0:T(8,128)(2,1)}, bf16[1,3,2,48,384]{4,3,2,1,0:T(8,128)(2,1)}, u32[]{:S(2)}, u32[]{:S(2)}) collective-permute-start(bf16[1,3,2,48,384]{4,3,2,1,0:T(8,128)(2,1)} %get-tuple-element.12), channel_id=1, source_target_pairs={{0,6},{1,7},{2,0},{3,1},{4,2},{5,3},{6,4},{7,5},{8,14},{9,15},{10,... | collective-permute-start | bytes 663560 | tf_op jit(solution)/shard_map/ppermute | solution.py:71
  149.1 36.7 %collective-permute-start.8 = (bf16[1,3,2,48,384]{4,3,2,1,0:T(8,128)(2,1)}, bf16[1,3,2,48,384]{4,3,2,1,0:T(8,128)(2,1)S(1)}, u32[]{:S(2)}, u32[]{:S(2)}) collective-permute-start(bf16[1,3,2,48,384]{4,3,2,1,0:T(8,128)(2,1)} %get-tuple-element.7), channel_id=1, source_target_pairs={{0,1},{1,2},{2,3},{3,4},{4,5},{5,6},{6,7},{7,0},{8,9},{9,10},{10,1... | collective-permute-start | bytes 663560 | tf_op jit(solution)/shard_map/ppermute | solution.py:71
  149.3 36.4 %collective-permute-start.7 = (bf16[1,3,2,48,384]{4,3,2,1,0:T(8,128)(2,1)}, bf16[1,3,2,48,384]{4,3,2,1,0:T(8,128)(2,1)S(1)}, u32[]{:S(2)}, u32[]{:S(2)}) collective-permute-start(bf16[1,3,2,48,384]{4,3,2,1,0:T(8,128)(2,1)} %get-tuple-element.8), channel_id=1, source_target_pairs={{0,2},{1,3},{2,4},{3,5},{4,6},{5,7},{6,0},{7,1},{8,10},{9,11},{10,... | collective-permute-start | bytes 663560 | tf_op jit(solution)/shard_map/ppermute | solution.py:71
  149.9 35.7 %collective-permute-start.6 = (bf16[1,3,2,48,384]{4,3,2,1,0:T(8,128)(2,1)}, bf16[1,3,2,48,384]{4,3,2,1,0:T(8,128)(2,1)S(1)}, u32[]{:S(2)}, u32[]{:S(2)}) collective-permute-start(bf16[1,3,2,48,384]{4,3,2,1,0:T(8,128)(2,1)} %get-tuple-element.9), channel_id=1, source_target_pairs={{0,3},{1,4},{2,5},{3,6},{4,7},{5,0},{6,1},{7,2},{8,11},{9,12},{10,... | collective-permute-start | bytes 663560 | tf_op jit(solution)/shard_map/ppermute | solution.py:71
  153.3 19.0 %collective-permute-start.4 = (bf16[1,3,2,48,384]{4,3,2,1,0:T(8,128)(2,1)}, bf16[1,3,2,48,384]{4,3,2,1,0:T(8,128)(2,1)S(1)}, u32[]{:S(2)}, u32[]{:S(2)}) collective-permute-start(bf16[1,3,2,48,384]{4,3,2,1,0:T(8,128)(2,1)} %get-tuple-element.11), channel_id=1, source_target_pairs={{0,5},{1,6},{2,7},{3,0},{4,1},{5,2},{6,3},{7,4},{8,13},{9,14},{10,... | collective-permute-start | bytes 663560 | tf_op jit(solution)/shard_map/ppermute | solution.py:71
  168.1 17.5 %collective-permute-start.5 = (bf16[1,3,2,48,384]{4,3,2,1,0:T(8,128)(2,1)}, bf16[1,3,2,48,384]{4,3,2,1,0:T(8,128)(2,1)S(1)}, u32[]{:S(2)}, u32[]{:S(2)}) collective-permute-start(bf16[1,3,2,48,384]{4,3,2,1,0:T(8,128)(2,1)} %get-tuple-element.10), channel_id=1, source_target_pairs={{0,4},{1,5},{2,6},{3,7},{4,0},{5,1},{6,2},{7,3},{8,12},{9,13},{10,... | collective-permute-start | bytes 663560 | tf_op jit(solution)/shard_map/ppermute | solution.py:71
